TPU v7x, 32 devices: a whole 2x2x4 slice. The times are simulated.
32 devices in a mesh: rep: 16 (over z, x, core), shard: 2 (over y).
Axes of the slice: x: 2, y: 2, z: 4, core: 2. Of those that a mesh axis runs over, the one named last changes fastest.
Arguments:
- tokens: bfloat16 [32, 197, 512], P(('rep', 'shard')), may hold values from -6 to 6
- norm_one: bfloat16 [512], P('shard'), may hold values from 0.099609375 to 1.8984375
- w_qkv: bfloat16 [512, 1536], P('shard'), may hold values from -0.25 to 0.25
- w_attn: bfloat16 [512, 512], P('shard'), may hold values from -1 to 1
- norm_two: bfloat16 [512], P('shard'), may hold values from 0.099609375 to 1.8984375
- w_gate: bfloat16 [512, 4], P('shard'), may hold values from -0.1875 to 0.1875
- w_expin: bfloat16 [4, 512, 2048], P(None, 'shard'), may hold values from -0.25 to 0.25
- w_expout: bfloat16 [4, 2048, 512], P(None, 'shard'), may hold values from -0.125 to 0.125
- routes: int32 [32, 197, 2], P(('rep', 'shard')), may hold values from 0 to 3, all different within a row
- cotangent: bfloat16 [32, 197, 512], P(('rep', 'shard')), may hold values from -6 to 6
Outputs:
- output: bfloat16 [32, 197, 512], P(('rep', 'shard'))
- grad_tokens: bfloat16 [32, 197, 512], P(('rep', 'shard'))
- grad_norm_one: float32 [512], P('shard')
- grad_qkv: float32 [512, 1536], P('shard')
- grad_attn: float32 [512, 512], P('shard')
- grad_norm_two: float32 [512], P('shard')
- grad_gate: float32 [512, 4], P('shard')
- grad_expin: float32 [4, 512, 2048], P(None, 'shard')
- grad_expout: float32 [4, 2048, 512], P(None, 'shard')
Inputs may be any that keep to these rules, and one draw needn't show every extreme that they name: `routes`: each token names two different experts; every expert is named by some token.
All inputs are finite; a program needn't handle non-finite values.
Results may differ from a plain program's by a relative error of at most 0.024.
Values may be sent and summed in bfloat16 or wider, within the bound.
A program may use at most 192 MiB of HBM per device.

v0:
```python
from functools import partial
import jax
import jax.numpy as jnp
from jax import lax
from jax.sharding import PartitionSpec as P

HEADS = 8
HEAD_DIM = 64
norm_eps = 1e-06
highest = lax.Precision.HIGHEST
fdt = jnp.float32
bdt = jnp.bfloat16


def layer_norm(inputs, gain_vec):
    centre = inputs - jnp.mean(inputs, axis=-1, keepdims=True)
    variance = jnp.mean(centre * centre, axis=-1, keepdims=True)
    inv_root = lax.rsqrt(variance + norm_eps)
    normed = centre * inv_root
    return (normed * gain_vec, normed, inv_root)


def norm_back(grad_out, normed, inv_root, gain_vec):
    scaled = grad_out * gain_vec
    back = inv_root * (
        scaled
        - jnp.mean(scaled, axis=-1, keepdims=True)
        - normed * jnp.mean(scaled * normed, axis=-1, keepdims=True)
    )
    return (back, jnp.sum(grad_out * normed, axis=0))


def forward(weights, tokens, routes, kept_total):
    norm_one, w_qkv, w_attn, norm_two, w_gate, w_expin, w_expout = weights
    images, seq_len, model_width = tokens.shape
    tok_rows = images * seq_len
    resid = tokens.reshape(tok_rows, model_width).astype(fdt)
    hidden_one, normed_one, root_one = layer_norm(resid, norm_one.astype(fdt))
    hidden_one_low = hidden_one.astype(bdt)
    proj = jnp.dot(hidden_one_low, w_qkv, preferred_element_type=fdt).astype(bdt)
    proj = proj.reshape(images, seq_len, 3, HEADS, HEAD_DIM)
    queries = proj[:, :, 0]
    key_rows = proj[:, :, 1]
    val_rows = proj[:, :, 2]
    score_scale = HEAD_DIM ** (-0.5)
    scores = (
        jnp.einsum("ishd,ithd->ihst", queries, key_rows, preferred_element_type=fdt) * score_scale
    )
    if kept_total is None:
        log_total = jax.nn.logsumexp(scores, axis=-1, keepdims=True)
    else:
        log_total = kept_total
    soft_probs = jnp.exp(scores - log_total)
    probs_low = soft_probs.astype(bdt)
    attn_rows = jnp.einsum("ihst,ithd->ishd", probs_low, val_rows, preferred_element_type=fdt)
    attn_rows = attn_rows.reshape(tok_rows, model_width).astype(bdt)
    mixed = resid + jnp.dot(attn_rows, w_attn, preferred_element_type=fdt)
    gate_gain = norm_two.astype(fdt)
    hidden_two, normed_two, root_two = layer_norm(mixed, gate_gain)
    router = w_gate.astype(fdt)
    logits = jnp.dot(hidden_two, router, precision=highest)
    expert_count = router.shape[1]
    choose = (
        routes.reshape(tok_rows, 2)[:, :, None] == jnp.arange(expert_count)[None, None, :]
    ).astype(fdt)
    picked = jnp.sum(choose * logits[:, None, :], axis=-1)
    gates = jax.nn.softmax(picked, axis=-1)
    weight_map = jnp.sum(gates[:, :, None] * choose, axis=1)
    hidden_two_low = hidden_two.astype(bdt)
    expert_inner = jnp.einsum("td,edf->etf", hidden_two_low, w_expin, preferred_element_type=fdt)
    hidden_act = jax.nn.gelu(expert_inner, approximate=False).astype(bdt)
    outer = jnp.einsum("etf,efd->etd", hidden_act, w_expout, preferred_element_type=fdt)
    combined = mixed + jnp.sum(weight_map.T[:, :, None] * outer, axis=0)
    return {
        "combined": combined,
        "log_total": log_total,
        "resid": resid,
        "normed_one": normed_one,
        "root_one": root_one,
        "hidden_one_low": hidden_one_low,
        "queries": queries,
        "key_rows": key_rows,
        "val_rows": val_rows,
        "soft_probs": soft_probs,
        "probs_low": probs_low,
        "attn_rows": attn_rows,
        "normed_two": normed_two,
        "root_two": root_two,
        "hidden_two": hidden_two,
        "hidden_two_low": hidden_two_low,
        "choose": choose,
        "gates": gates,
        "weight_map": weight_map,
        "expert_inner": expert_inner,
        "hidden_act": hidden_act,
        "outer": outer,
    }


def on_device(
    tokens, norm_one, w_qkv, w_attn, norm_two, w_gate, w_expin, w_expout, routes, cotangent
):
    images, seq_len, model_width = tokens.shape
    tok_rows = images * seq_len
    whole = (
        lax.all_gather(norm_one, "shard", axis=0, tiled=True),
        lax.all_gather(w_qkv, "shard", axis=0, tiled=True),
        lax.all_gather(w_attn, "shard", axis=0, tiled=True),
        lax.all_gather(norm_two, "shard", axis=0, tiled=True),
        lax.all_gather(w_gate, "shard", axis=0, tiled=True),
        lax.all_gather(w_expin, "shard", axis=1, tiled=True),
        lax.all_gather(w_expout, "shard", axis=1, tiled=True),
    )
    first = forward(whole, tokens, routes, None)
    output = first["combined"].reshape(images, seq_len, model_width).astype(bdt)
    again = (
        lax.all_gather(norm_one, "shard", axis=0, tiled=True),
        lax.all_gather(w_qkv, "shard", axis=0, tiled=True),
        lax.all_gather(w_attn, "shard", axis=0, tiled=True),
        lax.all_gather(norm_two, "shard", axis=0, tiled=True),
        lax.all_gather(w_gate, "shard", axis=0, tiled=True),
        lax.all_gather(w_expin, "shard", axis=1, tiled=True),
        lax.all_gather(w_expout, "shard", axis=1, tiled=True),
    )
    parts = forward(again, tokens, routes, first["log_total"])
    g_one, m_qkv, m_attn, g_two, m_gate, m_expin, m_expout = again
    gain_one = g_one.astype(fdt)
    gain_two = g_two.astype(fdt)
    router = m_gate.astype(fdt)
    dout = cotangent.reshape(tok_rows, model_width).astype(fdt)
    dweight = jnp.sum(dout[None, :, :] * parts["outer"], axis=-1).T
    dout_exp = (parts["weight_map"].T[:, :, None] * dout[None, :, :]).astype(bdt)
    grad_expout = jnp.einsum(
        "etf,etd->efd", parts["hidden_act"], dout_exp, preferred_element_type=fdt
    )
    dhidden = jnp.einsum("etd,efd->etf", dout_exp, m_expout, preferred_element_type=fdt)
    gelu_exact = partial(jax.nn.gelu, approximate=False)
    _, gelu_pull = jax.vjp(gelu_exact, parts["expert_inner"])
    dinner = gelu_pull(dhidden)[0].astype(bdt)
    grad_expin = jnp.einsum(
        "td,etf->edf", parts["hidden_two_low"], dinner, preferred_element_type=fdt
    )
    dhidden_two = jnp.einsum("etf,edf->td", dinner, m_expin, preferred_element_type=fdt)
    choose = parts["choose"]
    gates = parts["gates"]
    dpicked = jnp.sum(choose * dweight[:, None, :], axis=-1)
    gate_dot = jnp.sum(gates * dpicked, axis=-1, keepdims=True)
    dpair = gates * (dpicked - gate_dot)
    dlogits = jnp.sum(dpair[:, :, None] * choose, axis=1)
    grad_gate = jnp.dot(parts["hidden_two"].T, dlogits, precision=highest)
    dhidden_two = dhidden_two + jnp.dot(dlogits, router.T, precision=highest)
    dmixed_norm, grad_norm_two = norm_back(
        dhidden_two, parts["normed_two"], parts["root_two"], gain_two
    )
    dmixed = dout + dmixed_norm
    dmixed_low = dmixed.astype(bdt)
    grad_attn = jnp.dot(parts["attn_rows"].T, dmixed_low, preferred_element_type=fdt)
    dattn = jnp.dot(dmixed_low, m_attn.T, preferred_element_type=fdt).astype(bdt)
    dattn = dattn.reshape(images, seq_len, HEADS, HEAD_DIM)
    dprobs = jnp.einsum("ishd,ithd->ihst", dattn, parts["val_rows"], preferred_element_type=fdt)
    dvalues = jnp.einsum("ihst,ishd->ithd", parts["probs_low"], dattn, preferred_element_type=fdt)
    soft_probs = parts["soft_probs"]
    row_delta = jnp.sum(dprobs * soft_probs, axis=-1, keepdims=True)
    dscores = (soft_probs * (dprobs - row_delta)).astype(bdt)
    score_scale = HEAD_DIM ** (-0.5)
    dqueries = (
        jnp.einsum("ihst,ithd->ishd", dscores, parts["key_rows"], preferred_element_type=fdt)
        * score_scale
    )
    dkeys = (
        jnp.einsum("ihst,ishd->ithd", dscores, parts["queries"], preferred_element_type=fdt)
        * score_scale
    )
    dproj = (
        jnp.stack([dqueries, dkeys, dvalues], axis=2).reshape(tok_rows, 3 * model_width).astype(bdt)
    )
    grad_qkv = jnp.dot(parts["hidden_one_low"].T, dproj, preferred_element_type=fdt)
    dhidden_one = jnp.dot(dproj, m_qkv.T, preferred_element_type=fdt)
    dresid_norm, grad_norm_one = norm_back(
        dhidden_one, parts["normed_one"], parts["root_one"], gain_one
    )
    grad_tokens = (dmixed + dresid_norm).reshape(images, seq_len, model_width).astype(bdt)
    owned = (
        lax.psum_scatter(
            grad_norm_one.astype(jnp.bfloat16), "shard", scatter_dimension=0, tiled=True
        ).astype(jnp.float32),
        lax.psum_scatter(
            grad_qkv.astype(jnp.bfloat16), "shard", scatter_dimension=0, tiled=True
        ).astype(jnp.float32),
        lax.psum_scatter(
            grad_attn.astype(jnp.bfloat16), "shard", scatter_dimension=0, tiled=True
        ).astype(jnp.float32),
        lax.psum_scatter(
            grad_norm_two.astype(jnp.bfloat16), "shard", scatter_dimension=0, tiled=True
        ).astype(jnp.float32),
        lax.psum_scatter(
            grad_gate.astype(jnp.bfloat16), "shard", scatter_dimension=0, tiled=True
        ).astype(jnp.float32),
        lax.psum_scatter(
            grad_expin.astype(jnp.bfloat16), "shard", scatter_dimension=1, tiled=True
        ).astype(jnp.float32),
        lax.psum_scatter(
            grad_expout.astype(jnp.bfloat16), "shard", scatter_dimension=1, tiled=True
        ).astype(jnp.float32),
    )
    summed = (
        lax.psum(owned[0].astype(jnp.bfloat16), "rep").astype(jnp.float32),
        lax.psum(owned[1].astype(jnp.bfloat16), "rep").astype(jnp.float32),
        lax.psum(owned[2].astype(jnp.bfloat16), "rep").astype(jnp.float32),
        lax.psum(owned[3].astype(jnp.bfloat16), "rep").astype(jnp.float32),
        lax.psum(owned[4].astype(jnp.bfloat16), "rep").astype(jnp.float32),
        lax.psum(owned[5].astype(jnp.bfloat16), "rep").astype(jnp.float32),
        lax.psum(owned[6].astype(jnp.bfloat16), "rep").astype(jnp.float32),
    )
    return (
        output,
        grad_tokens,
        summed[0],
        summed[1],
        summed[2],
        summed[3],
        summed[4],
        summed[5],
        summed[6],
    )


def solution(mesh):
    placed = (
        P(("rep", "shard"), None, None),
        P("shard"),
        P("shard", None),
        P("shard", None),
        P("shard"),
        P("shard", None),
        P(None, "shard", None),
        P(None, "shard", None),
        P(("rep", "shard"), None, None),
        P(("rep", "shard"), None, None),
    )
    return jax.shard_map(
        on_device,
        mesh=mesh,
        in_specs=placed,
        out_specs=(
            P(("rep", "shard"), None, None),
            P(("rep", "shard"), None, None),
            P("shard"),
            P("shard", None),
            P("shard", None),
            P("shard"),
            P("shard", None),
            P(None, "shard", None),
            P(None, "shard", None),
        ),
        check_vma=False,
    )
```

profile of v0, /device:TPU:0, one launch (start us, length us, event | category | flops | bytes accessed | tf_op | source)
XLA Modules:
  0.0 764.5 jit_solution(5038029769242780368)
XLA Ops:
  9.7 5.2 all-gather
  14.8 4.2 all-gather.1
  19.1 4.3 all_gather.32
  23.7 14.0 %all_gather.30 = bf16[512,512]{1,0:T(8,128)(2,1)} all-gather(bf16[256,512]{1,0:T(8,128)(2,1)S(1)} %copy-done.11), channel_id=1, replica_groups=mesh['rep'=16,'shard'=2] {'shard'}, dimensions={0}, use_global_device_ids=true | all-gather | bytes 786432 | tf_op jit(solution)/shard_map/all_gather | solution.py:108
  38.5 6.7 all-gather.6.cloned.1.call-done
  45.2 1.9 convolution_convert_fusion.2
  49.3 1.4 fusion.76
  51.5 99.3 %all-gather.8.cloned.1.call-done = bf16[4,512,2048]{2,1,0:T(8,128)(2,1)} async-done(((bf16[4,256,2048]{2,1,0:T(8,128)(2,1)}), bf16[4,512,2048]{2,1,0:T(8,128)(2,1)}) %all-gather.8.cloned.1.call-update) | async-done | bytes 8388624 | tf_op jit(solution)/shard_map/all_gather | solution.py:111
  150.8 18.8 %fusion.2 = (bf16[4,197,2048]{2,1,0:T(8,128)(2,1)}, f32[4,197,2048]{2,1,0:T(8,128)}, f32[197,4,2048]{2,0,1:T(8,128)}) fusion(bf16[4,512,2048]{2,1,0:T(8,128)(2,1)} %all-gather.8.cloned.1.call-done, f32[512]{0:T(512)S(1)} %bitcast.219, f32[197]{0:T(256)S(1)} %add_rsqrt_fusion, f32[197,512]{1,0:T(8,128)S(1)} %get-tuple-element.69, ...), kind=kOutput, calls=%fused_computation.10 | convolution fusion | flops 1757857792 | bytes 24933928 | tf_op jit(solution)/shard_map/td,edf->etf/dot_general | solution.py:70
  169.6 86.8 %all-gather.10.cloned.1.call-done = bf16[4,2048,512]{2,1,0:T(8,128)(2,1)} async-done(((bf16[4,1024,512]{2,1,0:T(8,128)(2,1)}), bf16[4,2048,512]{2,1,0:T(8,128)(2,1)}) %all-gather.10.cloned.1.call-update) | async-done | bytes 8388624 | tf_op jit(solution)/shard_map/all_gather | solution.py:112
  256.4 6.5 multiply_reduce_fusion.1
  263.0 11.2 %fusion.8 = bf16[4,197,2048]{2,1,0:T(8,128)(2,1)S(1)} fusion(f32[4,197,2048]{2,1,0:T(8,128)} %get-tuple-element.63, f32[197,4,2048]{2,0,1:T(8,128)} %get-tuple-element.70, bf16[4,2048,512]{2,1,0:T(8,128)(2,1)} %all-gather.10.cloned.1.call-done, f32[197,512]{1,0:T(8,128)S(1)} %copy-done.6, f32[4,197]{1,0:T(4,128)S(1)} %bitcast.233), kind=kOutput, calls=%fused_computation.16 | convolution fusion | flops 1675956224 | bytes 24933456 | tf_op jit(solution)/shard_map/etd,efd->etf/dot_general | solution.py:136
  274.3 7.4 convolution_bitcast_fusion.1
  283.1 1.0 convolution_convert_fusion.5
  284.1 1.1 convolution_convert_fusion.3
  285.2 1.8 copy.52
  287.0 2.6 multiply_reduce_fusion
  289.9 1.9 multiply_convert_fusion
  293.0 1.9 convolution_convert_fusion.1
  295.0 8.1 %convert_bitcast_fusion = bf16[4,512,2048]{1,2,0:T(8,128)(2,1)} fusion(bf16[4,197,2048]{2,1,0:T(8,128)(2,1)} %copy-done.1, f32[512]{0:T(512)S(1)} %bitcast.222, f32[197,512]{1,0:T(8,128)S(1)} %get-tuple-element.69, f32[197]{0:T(256)S(1)} %add_rsqrt_fusion, f32[197]{0:T(256)S(1)} %broadcast_multiply_fusion.4), kind=kOutput, calls=%fused_computation.1 | convolution fusion | flops 1657153536 | bytes 12023336 | tf_op jit(solution)/shard_map/td,etf->edf/dot_general | solution.py:140
  304.1 7.9 %convolution_convert_fusion = bf16[4,2048,512]{2,1,0:T(8,128)(2,1)} fusion(bf16[4,197,2048]{2,1,0:T(8,128)(2,1)} %get-tuple-element.62, f32[197,512]{1,0:T(8,128)S(1)} %copy-done.7, f32[4,197]{1,0:T(4,128)S(1)} %bitcast.234), kind=kOutput, calls=%fused_computation.30 | convolution fusion | flops 1657556992 | bytes 12022864 | tf_op jit(solution)/shard_map/etf,etd->efd/dot_general | solution.py:133
  313.4 19.7 %reduce-scatter.8.cloned.1.call-done = bf16[256,1536]{1,0:T(8,128)(2,1)} async-done(((bf16[512,1536]{1,0:T(8,128)(2,1)}), bf16[256,1536]{1,0:T(8,128)(2,1)}) %reduce-scatter.8.cloned.1.call-update) | async-done | bytes 786448 | tf_op jit(solution)/shard_map/reduce_scatter | solution.py:187
  333.2 102.0 %reduce-scatter.12.cloned.1.call-done = bf16[4,256,2048]{1,2,0:T(8,128)(2,1)} async-done(((bf16[4,512,2048]{1,2,0:T(8,128)(2,1)}), bf16[4,256,2048]{1,2,0:T(8,128)(2,1)}) %reduce-scatter.12.cloned.1.call-update) | async-done | bytes 4194320 | tf_op jit(solution)/shard_map/reduce_scatter | solution.py:199
  435.2 102.2 %reduce-scatter.14.cloned.1.call-done = bf16[4,1024,512]{2,1,0:T(8,128)(2,1)} async-done(((bf16[4,2048,512]{2,1,0:T(8,128)(2,1)}), bf16[4,1024,512]{2,1,0:T(8,128)(2,1)}) %reduce-scatter.14.cloned.1.call-update) | async-done | bytes 4194320 | tf_op jit(solution)/shard_map/reduce_scatter | solution.py:202
  539.5 4.9 all-reduce.4
  545.5 4.4 reduce-scatter.16.cloned.1.call-done
  550.9 34.5 %all-reduce.2 = (bf16[256]{0:T(256)(128)(2,1)S(1)}, bf16[256]{0:T(256)(128)(2,1)S(1)}, bf16[256,4]{0,1:T(4,128)(2,1)S(1)}) all-reduce(bf16[256]{0:T(256)(128)(2,1)S(1)} %dynamic-slice.1, bf16[256]{0:T(256)(128)(2,1)S(1)} %dynamic-slice.3, bf16[256,4]{0,1:T(4,128)(2,1)S(1)} %copy.62), channel_id=1, replica_groups=mesh['rep'=16,'shard'=2] {'rep'}, use_global_device_ids=true, to_apply=%region_22.0 | all-reduce | flops 1536 | bytes 6144 | tf_op jit(solution)/shard_map/psum | solution.py:207
  587.1 153.0 %all-reduce.7.cloned.1.call-done = (bf16[4,256,2048]{1,2,0:T(8,128)(2,1)}, bf16[256,1536]{1,0:T(8,128)(2,1)}, bf16[256,512]{1,0:T(8,128)(2,1)}, bf16[4,1024,512]{2,1,0:T(8,128)(2,1)}) async-done(((bf16[4,256,2048]{1,2,0:T(8,128)(2,1)}, bf16[256,1536]{1,0:T(8,128)(2,1)}, bf16[256,512]{1,0:T(8,128)(2,1)}, bf16[4,1024,512]{2,1,0:T(8,128)(2,1)}), (bf16[4,256,2048]{1,2,0:T(8,128)(2,1)}, ...) | async-done | bytes 9437200 | tf_op jit(solution)/shard_map/psum | solution.py:212
  740.0 2.5 convert_element_type.206
  742.5 1.8 convert_element_type.208
  744.3 6.9 copy.56
  751.2 6.8 convert_element_type.217
  (101 shorter events, 16.9 us)
Async XLA Ops:
  7.2 2.3 copy-start
  7.2 2.4 copy-start.14
  7.2 7.6 copy-start.15
  7.2 11.9 %copy-start.13 = (bf16[256,4]{0,1:T(4,128)(2,1)S(1)}, bf16[256,4]{0,1:T(4,128)(2,1)}, u32[]{:S(2)}) copy-start(bf16[256,4]{0,1:T(4,128)(2,1)} %param.15) | copy-start | bytes 6148
  7.2 16.4 %copy-start.11 = (bf16[256,512]{1,0:T(8,128)(2,1)S(1)}, bf16[256,512]{1,0:T(8,128)(2,1)}, u32[]{:S(2)}) copy-start(bf16[256,512]{1,0:T(8,128)(2,1)} %param.13) | copy-start | bytes 786436
  7.2 30.5 %copy-start.9 = (bf16[1,197,512]{2,1,0:T(8,128)(2,1)S(1)}, bf16[1,197,512]{2,1,0:T(8,128)(2,1)}, u32[]{:S(2)}) copy-start(bf16[1,197,512]{2,1,0:T(8,128)(2,1)} %param.19) | copy-start | bytes 605188
  7.2 38.0 %all-gather.6.cloned.1.call-start = ((), (), s32[]{:S(2)}) async-start(), calls=%async_computation.5 | async-start | bytes 2359296 | tf_op jit(solution)/shard_map/all_gather | solution.py:107
  8.0 142.8 %all-gather.8.cloned.1.call-start = ((), (), s32[]{:S(2)}) async-start(), calls=%async_computation.6 | async-start | bytes 12582912 | tf_op jit(solution)/shard_map/all_gather | solution.py:111
  8.7 247.7 %all-gather.10.cloned.1.call-start = ((), (), s32[]{:S(2)}) async-start(), calls=%async_computation.7 | async-start | bytes 12582912 | tf_op jit(solution)/shard_map/all_gather | solution.py:112
  9.5 304.0 %reduce-scatter.10.cloned.1.call-start = ((), (), s32[]{:S(2)}) async-start(), calls=%async_computation.9 | async-start | bytes 786432 | tf_op jit(solution)/shard_map/reduce_scatter | solution.py:190
  23.7 27.7 %copy-start.12 = (s32[1,197,2]{1,2,0:T(2,128)S(1)}, s32[1,197,2]{1,2,0:T(2,128)}, u32[]{:S(2)}) copy-start(s32[1,197,2]{1,2,0:T(2,128)} %param.18) | copy-start | bytes 4732
  48.6 0.7 copy-start.3
  51.5 204.9 %copy-start.6 = (f32[197,512]{1,0:T(8,128)S(1)}, f32[197,512]{1,0:T(8,128)}, u32[]{:S(2)}) copy-start(f32[197,512]{1,0:T(8,128)} %bitcast_convert_fusion) | copy-start | bytes 1210372
  274.2 7.5 copy-start.1
  274.2 8.1 %copy-start.10 = (bf16[1,197,512]{2,1,0:T(8,128)(2,1)S(1)}, bf16[1,197,512]{2,1,0:T(8,128)(2,1)}, u32[]{:S(2)}) copy-start(bf16[1,197,512]{2,1,0:T(8,128)(2,1)} %param.19) | copy-start | bytes 605188
  274.2 8.9 %copy-start.2 = (bf16[512,512]{1,0:T(8,128)(2,1)S(1)}, bf16[512,512]{1,0:T(8,128)(2,1)}, u32[]{:S(2)}) copy-start(bf16[512,512]{1,0:T(8,128)(2,1)} %all_gather.30) | copy-start | bytes 1572868
  274.2 9.9 %copy-start.4 = (bf16[8,64,197]{2,1,0:T(8,128)(2,1)S(1)}, bf16[8,64,197]{2,1,0:T(8,128)(2,1)}, u32[]{:S(2)}) copy-start(bf16[8,64,197]{2,1,0:T(8,128)(2,1)} %copy-done.3) | copy-start | bytes 605188
  289.6 43.6 %reduce-scatter.8.cloned.1.call-start = ((), (), s32[]{:S(2)}) async-start(), calls=%async_computation.8 | async-start | bytes 2359296 | tf_op jit(solution)/shard_map/reduce_scatter | solution.py:187
  289.8 2.6 copy-start.5
  294.9 140.2 %reduce-scatter.12.cloned.1.call-start = ((), (), s32[]{:S(2)}) async-start(), calls=%async_computation.10 | async-start | bytes 12582912 | tf_op jit(solution)/shard_map/reduce_scatter | solution.py:199
  303.1 1.0 copy-start.7
  303.1 234.3 %reduce-scatter.14.cloned.1.call-start = ((), (), s32[]{:S(2)}) async-start(), calls=%async_computation.11 | async-start | bytes 12582912 | tf_op jit(solution)/shard_map/reduce_scatter | solution.py:202
  312.0 225.4 %copy-start.16 = (u32[32]{0:T(128)S(1)}, u32[32]{0:T(128)}, u32[]{:S(2)}) copy-start(u32[32]{0:T(128)} %constant.92) | copy-start | bytes 388
  312.0 226.7 %copy-start.8 = (bf16[512,1536]{1,0:T(8,128)(2,1)S(1)}, bf16[512,1536]{1,0:T(8,128)(2,1)}, u32[]{:S(2)}) copy-start(bf16[512,1536]{1,0:T(8,128)(2,1)} %all-gather.6.cloned.1.call-done) | copy-start | bytes 4718596
  312.0 237.9 %reduce-scatter.16.cloned.1.call-start = ((), (), s32[]{:S(2)}) async-start(), calls=%async_computation.12 | async-start | bytes 196608
  313.3 426.7 %all-reduce.7.cloned.1.call-start = ((), (), s32[]{:S(2)}) async-start(), calls=%async_computation.13 | async-start | bytes 18874368 | tf_op jit(solution)/shard_map/psum | solution.py:212
Sparse Core Ops, SparseCore 0:
  9.6 35.5 all-gather.5
  46.7 103.9 all-gather.7
  152.3 103.9 all-gather.9
  289.7 14.5 reduce-scatter.9
  307.0 26.0 reduce-scatter.7
  335.9 99.2 reduce-scatter.11
  438.1 99.2 reduce-scatter.13
  539.6 10.2 reduce-scatter.15
  553.9 186.0 all-reduce.6
where the time goes:
time: 765 us; the launch traced here: 764 us
  waiting for transfers between devices  576 us (75%)
  matrix products  74.1 us (10%)
  blocking collectives  67.2 us (9%)
  other arithmetic  18.4 us (2%)
  between operations  14.8 us (2%)
  local copies, waits for them, and re-layouts  13.1 us (2%)
    psum x1, waiting for transfers between devices, on_device(): lax.psum(owned[5].astype(jnp.bfloat16), 'rep').astype(jnp.float32)  153 us
    reduce_scatter x1, waiting for transfers between devices, on_device(): lax.psum_scatter(grad_expout.astype(jnp.bfloat16), 'shard', scatter_dimen...  102 us
    reduce_scatter x1, waiting for transfers between devices, on_device(): lax.psum_scatter(grad_expin.astype(jnp.bfloat16), 'shard', scatter_dimens...  102 us
    all_gather x1, waiting for transfers between devices, on_device(): lax.all_gather(w_expin, 'shard', axis=1, tiled=True)  99.3 us
    all_gather x1, waiting for transfers between devices, on_device(): lax.all_gather(w_expout, 'shard', axis=1, tiled=True)  86.8 us
    psum x1, blocking collectives, on_device(): lax.psum(owned[0].astype(jnp.bfloat16), 'rep').astype(jnp.float32)  34.5 us
    reduce_scatter x1, waiting for transfers between devices, on_device(): lax.psum_scatter(grad_qkv.astype(jnp.bfloat16), 'shard', scatter_dimensio...  19.7 us
    dot_general x1, matrix products, forward(): jnp.einsum('td,edf->etf', hidden_two_low, w_expin, preferred_element_type...  18.8 us
  transfers between devices with their start and end apart: 9, of which 8 were waited for; matrix products, arithmetic and copies ran while one was open for 7% of the time, Pallas kernels for 0%

commit v1 on v0

--- a/solution.py
+++ b/solution.py
@@ -10,6 +10,18 @@
 highest = lax.Precision.HIGHEST
 fdt = jnp.float32
 bdt = jnp.bfloat16
+
+
+def doubled_up(x, axis, dim):
+    ways, here, step = (lax.axis_size(axis), lax.axis_index(axis), x.shape[dim])
+    line, have = (x, 1)
+    while have < ways:
+        line = jnp.concatenate(
+            [line, lax.ppermute(line, axis, [(d, (d - have) % ways) for d in range(ways)])],
+            axis=dim,
+        )
+        have = 2 * have
+    return jnp.roll(line, here * step, axis=dim)
 
 
 def layer_norm(inputs, gain_vec):
@@ -109,7 +121,7 @@
         lax.all_gather(norm_two, "shard", axis=0, tiled=True),
         lax.all_gather(w_gate, "shard", axis=0, tiled=True),
         lax.all_gather(w_expin, "shard", axis=1, tiled=True),
-        lax.all_gather(w_expout, "shard", axis=1, tiled=True),
+        doubled_up(w_expout, "shard", 1),
     )
     first = forward(whole, tokens, routes, None)
     output = first["combined"].reshape(images, seq_len, model_width).astype(bdt)

time: 765 us -> 842 us (1.10)
  blocking collectives: 67.2 us -> 220 us
  waiting for transfers between devices: 576 us -> 487 us
  matrix products: 74.1 us -> 83.7 us
    all_gather x1, blocking collectives: 5.16 us -> 158 us  [on_device(): lax.all_gather(norm_one, 'shard', axis=0, tiled=True)]
    all_gather x1, waiting for transfers between devices: 99.3 us -> 15.8 us  [on_device(): lax.all_gather(w_expin, 'shard', axis=1, tiled=True)]
    dot_general x1 -> x2, matrix products: 6.5 us -> 16 us  [forward(): jnp.einsum('etf,efd->etd', hidden_act, w_expout, preferred_element_type=fdt)]
  transfers between devices with their start and end apart: 9 -> 10, of which waited for: 8 -> 7; matrix products, arithmetic and copies ran while one was open for 7% -> 9% of each run, Pallas kernels for 0% -> 0%
where the time goes in v1:
time: 842 us; the launch traced here: 841 us
  waiting for transfers between devices  487 us (58%)
  blocking collectives  220 us (26%)
  matrix products  83.7 us (10%)
  other arithmetic  18.3 us (2%)
  between operations  14.9 us (2%)
  local copies, waits for them, and re-layouts  13.1 us (2%)
    all_gather x1, blocking collectives, on_device(): lax.all_gather(norm_one, 'shard', axis=0, tiled=True)  158 us
    psum x1, waiting for transfers between devices, on_device(): lax.psum(owned[5].astype(jnp.bfloat16), 'rep').astype(jnp.float32)  153 us
    reduce_scatter x1, waiting for transfers between devices, on_device(): lax.psum_scatter(grad_expout.astype(jnp.bfloat16), 'shard', scatter_dimen...  102 us
    reduce_scatter x1, waiting for transfers between devices, on_device(): lax.psum_scatter(grad_expin.astype(jnp.bfloat16), 'shard', scatter_dimens...  102 us
    all_gather x1, waiting for transfers between devices, on_device(): lax.all_gather(w_expout, 'shard', axis=1, tiled=True)  88.2 us
    psum x1, blocking collectives, on_device(): lax.psum(owned[0].astype(jnp.bfloat16), 'rep').astype(jnp.float32)  34.5 us
    reduce_scatter x1, waiting for transfers between devices, on_device(): lax.psum_scatter(grad_qkv.astype(jnp.bfloat16), 'shard', scatter_dimensio...  19.7 us
    dot_general x1, matrix products, forward(): jnp.einsum('td,edf->etf', hidden_two_low, w_expin, preferred_element_type...  18.8 us
  transfers between devices with their start and end apart: 10, of which 7 were waited for; matrix products, arithmetic and copies ran while one was open for 9% of the time, Pallas kernels for 0%

profile of v1, /device:TPU:0, one launch (start us, length us, event | category | flops | bytes accessed | tf_op | source)
XLA Modules:
  0.0 840.8 jit_solution(4942526393530975611)
XLA Ops:
  9.5 3.0 collective-permute-start
  12.5 157.6 %all-gather = bf16[2,1,256]{2,1,0:T(2,128)(2,1)S(1)} all-gather(bf16[1,1,256]{2,1,0:T(2,128)(2,1)S(1)} %reshape.328), channel_id=1, replica_groups=mesh['rep'=16,'shard'=2] {'shard'}, dimensions={0}, use_global_device_ids=true | all-gather | bytes 1536 | tf_op jit(solution)/shard_map/all_gather | solution.py:118
  170.2 4.7 all-gather.1
  174.9 4.3 all_gather.31
  179.6 13.7 %all_gather.29 = bf16[512,512]{1,0:T(8,128)(2,1)} all-gather(bf16[256,512]{1,0:T(8,128)(2,1)S(1)} %copy-done.13), channel_id=1, replica_groups=mesh['rep'=16,'shard'=2] {'shard'}, dimensions={0}, use_global_device_ids=true | all-gather | bytes 786432 | tf_op jit(solution)/shard_map/all_gather | solution.py:120
  194.1 1.9 convolution_convert_fusion.2
  198.1 1.4 fusion.86
  200.2 15.8 %all-gather.8.cloned.1.call-done = bf16[4,512,2048]{2,1,0:T(8,128)(2,1)} async-done(((bf16[4,256,2048]{2,1,0:T(8,128)(2,1)}), bf16[4,512,2048]{2,1,0:T(8,128)(2,1)}) %all-gather.8.cloned.1.call-update) | async-done | bytes 8388624 | tf_op jit(solution)/shard_map/all_gather | solution.py:123
  216.0 18.8 %fusion.7 = (bf16[4,197,2048]{2,1,0:T(8,128)(2,1)}, f32[4,197,2048]{2,1,0:T(8,128)}, f32[197,4,2048]{2,0,1:T(8,128)}) fusion(bf16[4,512,2048]{2,1,0:T(8,128)(2,1)} %all-gather.8.cloned.1.call-done, f32[512]{0:T(512)S(1)} %bitcast.220, f32[197]{0:T(256)S(1)} %add_rsqrt_fusion, f32[197,512]{1,0:T(8,128)S(1)} %get-tuple-element.73, ...), kind=kOutput, calls=%fused_computation.18 | convolution fusion | flops 1757857792 | bytes 24933928 | tf_op jit(solution)/shard_map/td,edf->etf/dot_general | solution.py:82
  234.8 88.2 %all-gather.10.cloned.1.call-done = bf16[4,2048,512]{2,1,0:T(8,128)(2,1)} async-done(((bf16[4,1024,512]{2,1,0:T(8,128)(2,1)}), bf16[4,2048,512]{2,1,0:T(8,128)(2,1)}) %all-gather.10.cloned.1.call-update) | async-done | bytes 8388624 | tf_op jit(solution)/shard_map/all_gather | solution.py:135
  323.1 6.4 multiply_reduce_fusion.1
  329.6 11.2 %fusion.13 = bf16[4,197,2048]{2,1,0:T(8,128)(2,1)S(1)} fusion(f32[4,197,2048]{2,1,0:T(8,128)} %get-tuple-element.67, f32[197,4,2048]{2,0,1:T(8,128)} %get-tuple-element.74, bf16[4,2048,512]{2,1,0:T(8,128)(2,1)} %all-gather.10.cloned.1.call-done, f32[197,512]{1,0:T(8,128)S(1)} %copy-done.8, f32[4,197]{1,0:T(4,128)S(1)} %bitcast.229), kind=kOutput, calls=%fused_computation.24 | convolution fusion | flops 1675956224 | bytes 24933456 | tf_op jit(solution)/shard_map/etd,efd->etf/dot_general | solution.py:148
  340.9 7.4 convolution_bitcast_fusion.1
  348.9 9.7 %multiply_reduce_fusion.2 = f32[197,512]{1,0:T(8,128)S(1)} fusion(bf16[4,197,2048]{2,1,0:T(8,128)(2,1)S(1)} %copy-done.4, s32[]{:T(128)S(6)} %select_n.26, bf16[4,1024,512]{2,1,0:T(8,128)(2,1)S(1)} %copy-done.3, bf16[4,1024,512]{2,1,0:T(8,128)(2,1)} %collective-permute-done, f32[4,197]{1,0:T(4,128)S(1)} %bitcast.230), kind=kOutput, calls=%fused_computation.45 | convolution fusion | flops 1686816256 | bytes 12022868 | tf_op jit(solution)/shard_map/etf,efd->etd/dot_general | solution.py:84
  360.5 1.1 convolution_convert_fusion.3
  361.6 1.8 copy.52
  363.3 2.6 multiply_reduce_fusion
  366.0 1.9 multiply_convert_fusion
  369.1 1.9 convolution_convert_fusion.1
  371.1 8.2 convert_bitcast_fusion
  380.3 7.9 convolution_convert_fusion
  389.9 19.7 %reduce-scatter.8.cloned.1.call-done = bf16[256,1536]{1,0:T(8,128)(2,1)} async-done(((bf16[512,1536]{1,0:T(8,128)(2,1)}), bf16[256,1536]{1,0:T(8,128)(2,1)}) %reduce-scatter.8.cloned.1.call-update) | async-done | bytes 786448 | tf_op jit(solution)/shard_map/reduce_scatter | solution.py:199
  409.5 102.0 %reduce-scatter.12.cloned.1.call-done = bf16[4,256,2048]{1,2,0:T(8,128)(2,1)} async-done(((bf16[4,512,2048]{1,2,0:T(8,128)(2,1)}), bf16[4,256,2048]{1,2,0:T(8,128)(2,1)}) %reduce-scatter.12.cloned.1.call-update) | async-done | bytes 4194320 | tf_op jit(solution)/shard_map/reduce_scatter | solution.py:211
  511.5 102.2 %reduce-scatter.14.cloned.1.call-done = bf16[4,1024,512]{2,1,0:T(8,128)(2,1)} async-done(((bf16[4,2048,512]{2,1,0:T(8,128)(2,1)}), bf16[4,1024,512]{2,1,0:T(8,128)(2,1)}) %reduce-scatter.14.cloned.1.call-update) | async-done | bytes 4194320 | tf_op jit(solution)/shard_map/reduce_scatter | solution.py:214
  615.9 4.9 all-reduce.4
  621.9 4.4 reduce-scatter.16.cloned.1.call-done
  627.2 34.5 %all-reduce.2 = (bf16[256]{0:T(256)(128)(2,1)S(1)}, bf16[256]{0:T(256)(128)(2,1)S(1)}, bf16[256,4]{0,1:T(4,128)(2,1)S(1)}) all-reduce(bf16[256]{0:T(256)(128)(2,1)S(1)} %dynamic-slice.1, bf16[256]{0:T(256)(128)(2,1)S(1)} %dynamic-slice.3, bf16[256,4]{0,1:T(4,128)(2,1)S(1)} %copy.62), channel_id=1, replica_groups=mesh['rep'=16,'shard'=2] {'rep'}, use_global_device_ids=true, to_apply=%region_22.23 | all-reduce | flops 1536 | bytes 6144 | tf_op jit(solution)/shard_map/psum | solution.py:219
  663.5 152.9 %all-reduce.7.cloned.1.call-done = (bf16[4,256,2048]{1,2,0:T(8,128)(2,1)}, bf16[256,1536]{1,0:T(8,128)(2,1)}, bf16[256,512]{1,0:T(8,128)(2,1)}, bf16[4,1024,512]{2,1,0:T(8,128)(2,1)}) async-done(((bf16[4,256,2048]{1,2,0:T(8,128)(2,1)}, bf16[256,1536]{1,0:T(8,128)(2,1)}, bf16[256,512]{1,0:T(8,128)(2,1)}, bf16[4,1024,512]{2,1,0:T(8,128)(2,1)}), (bf16[4,256,2048]{1,2,0:T(8,128)(2,1)}, ...) | async-done | bytes 9437200 | tf_op jit(solution)/shard_map/psum | solution.py:224
  816.4 2.5 convert_element_type.206
  818.8 1.8 convert_element_type.208
  820.6 6.9 copy.56
  827.5 6.8 convert_element_type.217
  (105 shorter events, 17.8 us)
Async XLA Ops:
  7.2 5.4 copy-start.16
  7.2 163.0 %copy-start.17 = (bf16[256]{0:T(256)(128)(2,1)S(1)}, bf16[256]{0:T(256)(128)(2,1)}, u32[]{:S(2)}) copy-start(bf16[256]{0:T(256)(128)(2,1)} %param.14) | copy-start | bytes 1540
  7.2 167.7 %copy-start.15 = (bf16[256,4]{0,1:T(4,128)(2,1)S(1)}, bf16[256,4]{0,1:T(4,128)(2,1)}, u32[]{:S(2)}) copy-start(bf16[256,4]{0,1:T(4,128)(2,1)} %param.15) | copy-start | bytes 6148
  7.2 172.0 %copy-start = (bf16[1,197,512]{2,1,0:T(8,128)(2,1)S(1)}, bf16[1,197,512]{2,1,0:T(8,128)(2,1)}, u32[]{:S(2)}) copy-start(bf16[1,197,512]{2,1,0:T(8,128)(2,1)} %param.10) | copy-start | bytes 605188
  7.2 172.3 %copy-start.13 = (bf16[256,512]{1,0:T(8,128)(2,1)S(1)}, bf16[256,512]{1,0:T(8,128)(2,1)}, u32[]{:S(2)}) copy-start(bf16[256,512]{1,0:T(8,128)(2,1)} %param.13) | copy-start | bytes 786436
  7.2 186.0 %copy-start.11 = (bf16[1,197,512]{2,1,0:T(8,128)(2,1)S(1)}, bf16[1,197,512]{2,1,0:T(8,128)(2,1)}, u32[]{:S(2)}) copy-start(bf16[1,197,512]{2,1,0:T(8,128)(2,1)} %param.19) | copy-start | bytes 605188
  7.2 186.8 %all-gather.6.cloned.1.call-start = ((), (), s32[]{:S(2)}) async-start(), calls=%async_computation.5 | async-start | bytes 2359296 | tf_op jit(solution)/shard_map/all_gather | solution.py:119
  8.0 208.0 %all-gather.8.cloned.1.call-start = ((), (), s32[]{:S(2)}) async-start(), calls=%async_computation.6 | async-start | bytes 12582912 | tf_op jit(solution)/shard_map/all_gather | solution.py:123
  8.7 314.4 %all-gather.10.cloned.1.call-start = ((), (), s32[]{:S(2)}) async-start(), calls=%async_computation.7 | async-start | bytes 12582912 | tf_op jit(solution)/shard_map/all_gather | solution.py:135
  9.5 380.4 %reduce-scatter.10.cloned.1.call-start = ((), (), s32[]{:S(2)}) async-start(), calls=%async_computation.9 | async-start | bytes 786432 | tf_op jit(solution)/shard_map/reduce_scatter | solution.py:202
  9.5 339.4 %collective-permute-start = (bf16[4,1024,512]{2,1,0:T(8,128)(2,1)}, bf16[4,1024,512]{2,1,0:T(8,128)(2,1)}, u32[]{:S(2)}, u32[]{:S(2)}) collective-permute-start(bf16[4,1024,512]{2,1,0:T(8,128)(2,1)} %param.17), channel_id=1, source_target_pairs={{0,1},{1,0},{2,3},{3,2},{4,5},{5,4},{6,7},{7,6},{8,9},{9,8},{10,11... | collective-permute-start | bytes 12582920 | tf_op jit(solution)/shard_map/ppermute | solution.py:20
  197.4 0.7 copy-start.5
  200.2 122.9 %copy-start.8 = (f32[197,512]{1,0:T(8,128)S(1)}, f32[197,512]{1,0:T(8,128)}, u32[]{:S(2)}) copy-start(f32[197,512]{1,0:T(8,128)} %bitcast_convert_fusion) | copy-start | bytes 1210372
  323.1 6.4 copy-start.14
  340.8 7.4 copy-start.1
  340.8 8.1 copy-start.3
  340.9 8.1 copy-start.4
  348.9 9.7 %copy-start.12 = (bf16[1,197,512]{2,1,0:T(8,128)(2,1)S(1)}, bf16[1,197,512]{2,1,0:T(8,128)(2,1)}, u32[]{:S(2)}) copy-start(bf16[1,197,512]{2,1,0:T(8,128)(2,1)} %param.19) | copy-start | bytes 605188
  348.9 10.6 %copy-start.2 = (bf16[512,512]{1,0:T(8,128)(2,1)S(1)}, bf16[512,512]{1,0:T(8,128)(2,1)}, u32[]{:S(2)}) copy-start(bf16[512,512]{1,0:T(8,128)(2,1)} %all_gather.29) | copy-start | bytes 1572868
  348.9 11.6 %copy-start.6 = (bf16[8,64,197]{2,1,0:T(8,128)(2,1)S(1)}, bf16[8,64,197]{2,1,0:T(8,128)(2,1)}, u32[]{:S(2)}) copy-start(bf16[8,64,197]{2,1,0:T(8,128)(2,1)} %copy-done.5) | copy-start | bytes 605188
  365.9 43.6 %reduce-scatter.8.cloned.1.call-start = ((), (), s32[]{:S(2)}) async-start(), calls=%async_computation.8 | async-start | bytes 2359296 | tf_op jit(solution)/shard_map/reduce_scatter | solution.py:199
  366.0 2.6 copy-start.7
  371.1 140.5 %reduce-scatter.12.cloned.1.call-start = ((), (), s32[]{:S(2)}) async-start(), calls=%async_computation.10 | async-start | bytes 12582912 | tf_op jit(solution)/shard_map/reduce_scatter | solution.py:211
  379.3 1.0 copy-start.9
  379.3 234.5 %reduce-scatter.14.cloned.1.call-start = ((), (), s32[]{:S(2)}) async-start(), calls=%async_computation.11 | async-start | bytes 12582912 | tf_op jit(solution)/shard_map/reduce_scatter | solution.py:214
  388.2 225.6 %copy-start.18 = (u32[32]{0:T(128)S(1)}, u32[32]{0:T(128)}, u32[]{:S(2)}) copy-start(u32[32]{0:T(128)} %constant.120) | copy-start | bytes 388
  388.2 226.9 %copy-start.10 = (bf16[512,1536]{1,0:T(8,128)(2,1)S(1)}, bf16[512,1536]{1,0:T(8,128)(2,1)}, u32[]{:S(2)}) copy-start(bf16[512,1536]{1,0:T(8,128)(2,1)} %all-gather.6.cloned.1.call-done) | copy-start | bytes 4718596
  388.2 238.1 %reduce-scatter.16.cloned.1.call-start = ((), (), s32[]{:S(2)}) async-start(), calls=%async_computation.12 | async-start | bytes 196608
  389.8 426.6 %all-reduce.7.cloned.1.call-start = ((), (), s32[]{:S(2)}) async-start(), calls=%async_computation.13 | async-start | bytes 18874368 | tf_op jit(solution)/shard_map/psum | solution.py:224
Sparse Core Ops, SparseCore 0:
  9.6 46.8 all-gather.5
  58.1 157.8 all-gather.7
  217.6 105.4 all-gather.9
  366.0 14.5 reduce-scatter.9
  383.4 26.0 reduce-scatter.7
  412.3 99.2 reduce-scatter.11
  514.5 99.2 reduce-scatter.13
  616.0 10.2 reduce-scatter.15
  630.3 186.0 all-reduce.6
